TPU v7x, 32 devices: a whole 2x2x4 slice. The times are simulated.
32 devices in a mesh: pol: 4 (over y, x), slab: 8 (over z, core).
Axes of the slice: x: 2, y: 2, z: 4, core: 2. Of those that a mesh axis runs over, the one named last changes fastest.
Arguments:
- correlations: bfloat16 [2, 4, 512, 256], P(None, 'pol', 'slab'), may hold values from -6 to 6
- tracks: float32 [3, 512, 256], P(None, 'slab'), may hold values from -1 to 1
- vis_counts: int32 [512], P('slab'), may hold values from 1 to 256
- offsets: int32 [2, 512], replicated, may hold values from 0 to 4064, as said below
- held_counts: int32 [8], replicated, may hold values from 1 to 64, as said below
- pixel_weight: float32 [32, 32], replicated, may hold values from 0.25 to 1
Outputs:
- sky_image: float32 [2, 4, 4096, 4096], P(None, 'pol', 'slab')
Inputs may be any that keep to these rules, and one draw needn't show every extreme that they name: A holder's live slots are its first held_counts ones; one holder holds 64. offsets[0, b] // 512 == b // 64: a subgrid starts in the row slab of its holder.
All inputs are finite; a program needn't handle non-finite values.
Results may differ from a plain program's by a relative error of at most 0.0039.
Values may be sent and summed in bfloat16 or wider, within the bound.
No kernel may reach another device: no remote copies, remote signals or barrier semaphores. Data moves between devices by JAX's collectives and lax.ppermute only.
A program may use at most 128 MiB of HBM per device.

v0:
```python
import math
import jax
import jax.numpy as jnp
import numpy as np
from jax import lax
from jax.sharding import PartitionSpec as P

G = 4096
SUB = 32
VIS = 256
SLOTS = 64
TWO_PI = 2.0 * math.pi
FIELD_VIEW = 0.6
DEPTH_SCALE = 40.0
TRACK_SCALE = 0.375
COEF_REAL = np.array(
    [[0.5, 0.0, 0.0, 0.5], [0.5, 0.0, 0.0, -0.5], [0.0, 0.5, 0.5, 0.0], [0.0, 0.0, 0.0, 0.0]],
    np.float32,
)
COEF_IMAG = np.array(
    [[0.0, 0.0, 0.0, 0.0], [0.0, 0.0, 0.0, 0.0], [0.0, 0.0, 0.0, 0.0], [0.0, -0.5, 0.5, 0.0]],
    np.float32,
)


def partner_2(value, axis, distance):
    return lax.ppermute(value, axis, [(i, i ^ 1 << distance) for i in range(lax.axis_size(axis))])


def passed_along(value, axis, by):
    peers = lax.axis_size(axis)
    pairs = [(i, i + by) for i in range(peers) if 0 <= i + by < peers]
    return lax.ppermute(value, axis, pairs)


def pixel_tables():
    cells = jnp.arange(SUB * SUB, dtype=jnp.int32)
    row_pos = (cells // SUB - SUB // 2).astype(jnp.float32) / SUB
    col_pos = (cells % SUB - SUB // 2).astype(jnp.float32) / SUB
    depth = jnp.sqrt(1.0 - (FIELD_VIEW * col_pos) ** 2 - (FIELD_VIEW * row_pos) ** 2) - 1.0
    return (col_pos, row_pos, depth)


def phasor_table(track_set, tables):
    col_pos, row_pos, depth = tables
    u_cells = track_set[0] * (TRACK_SCALE * SUB)
    v_cells = track_set[1] * (TRACK_SCALE * SUB)
    w_cells = track_set[2] * DEPTH_SCALE
    phase = TWO_PI * (
        u_cells[:, None] * col_pos[None, :]
        + v_cells[:, None] * row_pos[None, :]
        + w_cells[:, None] * depth[None, :]
    )
    return jnp.concatenate([jnp.cos(phase), jnp.sin(phase)], axis=1).astype(jnp.bfloat16)


def subgrid_tables():
    positions = jnp.arange(SUB, dtype=jnp.int32) - SUB // 2
    turn_count = positions[:, None] * positions[None, :] % SUB
    angles = -TWO_PI * turn_count.astype(jnp.float32) / SUB
    return (jnp.cos(angles), jnp.sin(angles))


def dft_table(length):
    positions = jnp.arange(length, dtype=jnp.int32)
    turn_count = positions[:, None] * positions[None, :] % length
    angles = TWO_PI * turn_count.astype(jnp.float32) / length
    return (jnp.cos(angles), jnp.sin(angles))


def twiddle_table(first_len, second_len, length):
    first_pos = jnp.arange(first_len, dtype=jnp.int32)
    second_pos = jnp.arange(second_len, dtype=jnp.int32)
    turn_count = first_pos[:, None] * second_pos[None, :] % length
    angles = TWO_PI * turn_count.astype(jnp.float32) / length
    return (jnp.cos(angles), jnp.sin(angles))


def complex_einsum(pattern, left_pair, right_pair):
    highest = lax.Precision.HIGHEST
    left_re, left_im = left_pair
    right_re, right_im = right_pair
    real_part = jnp.einsum(pattern, left_re, right_re, precision=highest) - jnp.einsum(
        pattern, left_im, right_im, precision=highest
    )
    imag_part = jnp.einsum(pattern, left_re, right_im, precision=highest) + jnp.einsum(
        pattern, left_im, right_re, precision=highest
    )
    return (real_part, imag_part)


def complex_multiply(data_pair, table_pair):
    data_re, data_im = data_pair
    table_re, table_im = table_pair
    return (data_re * table_re - data_im * table_im, data_re * table_im + data_im * table_re)


def subgrid_transform(sub_re, sub_im, dft_pair):
    half_re, half_im = complex_einsum("...ij,cj->...ic", (sub_re, sub_im), dft_pair)
    return complex_einsum("ai,...ic->...ac", dft_pair, (half_re, half_im))


def place_blocks(window, blocks, row_starts, col_starts):
    block_count = blocks.shape[1]
    zero_index = jnp.zeros((), jnp.int32)

    def add_one(slot_index, current_window):
        block = lax.dynamic_index_in_dim(blocks, slot_index, 1, keepdims=False)
        corner = (zero_index, row_starts[slot_index], col_starts[slot_index])
        current = lax.dynamic_slice(current_window, corner, (2, SUB, SUB))
        return lax.dynamic_update_slice(current_window, current + block, corner)

    return lax.fori_loop(0, block_count, add_one, window)


def on_device(correlations, tracks, vis_counts, offsets, held_counts, pixel_weight):
    highest = lax.Precision.HIGHEST
    slab_count = lax.axis_size("slab")
    slab_index = lax.axis_index("slab")
    stokes_index = lax.axis_index("pol")
    pixel_area = SUB * SUB
    rows_local = G // slab_count
    tables = pixel_tables()
    dft_pair = subgrid_tables()
    gathered = lax.all_gather(correlations, "pol", axis=1, tiled=True)
    corr_float = gathered.astype(jnp.float32)
    select = (jnp.arange(4, dtype=jnp.int32) == stokes_index).astype(jnp.float32)
    coef_re = jnp.sum(select[:, None] * jnp.asarray(COEF_REAL), axis=0)
    coef_im = jnp.sum(select[:, None] * jnp.asarray(COEF_IMAG), axis=0)
    stokes_re = jnp.einsum("p,pnv->nv", coef_re, corr_float[0], precision=highest) - jnp.einsum(
        "p,pnv->nv", coef_im, corr_float[1], precision=highest
    )
    stokes_im = jnp.einsum("p,pnv->nv", coef_re, corr_float[1], precision=highest) + jnp.einsum(
        "p,pnv->nv", coef_im, corr_float[0], precision=highest
    )
    visible = (jnp.arange(VIS, dtype=jnp.int32)[None, :] < vis_counts[:, None]).astype(jnp.bfloat16)
    stokes_vis = jnp.stack([stokes_re, stokes_im]).astype(jnp.bfloat16) * visible[None]
    holder_ids = jnp.arange(slab_count, dtype=jnp.int32)
    own_held = jnp.sum(jnp.where(holder_ids == slab_index, held_counts, 0))

    def grid_range(vis_set, track_set, first_slot, stop_slot, capacity):

        def one_slot(slot_index, subgrid_set):
            phasor = phasor_table(
                lax.dynamic_index_in_dim(track_set, slot_index, 1, keepdims=False), tables
            )
            vis_slot = lax.dynamic_index_in_dim(vis_set, slot_index, 1, keepdims=False)
            product = jnp.dot(vis_slot, phasor, preferred_element_type=jnp.float32)
            sub_re = product[0, :pixel_area] - product[1, pixel_area:]
            sub_im = product[0, pixel_area:] + product[1, :pixel_area]
            update = jnp.stack([sub_re, sub_im])[:, None, :]
            return lax.dynamic_update_slice_in_dim(subgrid_set, update, slot_index, 1)

        zero_set = jnp.zeros((2, capacity, pixel_area), jnp.float32)
        return lax.fori_loop(first_slot, stop_slot, one_slot, zero_set)

    half_slots = SLOTS // 2
    swap_bit = slab_count.bit_length() - 2
    partner = jnp.bitwise_xor(slab_index, slab_count // 2)
    partner_held = jnp.sum(jnp.where(holder_ids == partner, held_counts, 0))
    pair_total = own_held + partner_held
    own_give = jnp.maximum(own_held - (pair_total + 1) // 2, 0)
    partner_give = jnp.maximum(partner_held - (pair_total + 1) // 2, 0)
    own_start = jnp.minimum(own_held - own_give, SLOTS - half_slots)
    partner_start = jnp.minimum(partner_held - partner_give, SLOTS - half_slots)
    send_vis = lax.dynamic_slice_in_dim(stokes_vis, own_start, half_slots, 1).astype(jnp.float32)
    send_track = lax.dynamic_slice_in_dim(tracks, own_start, half_slots, 1)
    got_vis, got_track = partner_2((send_vis, send_track), "slab", swap_bit)
    first_slot = partner_held - partner_give - partner_start
    helped = grid_range(
        got_vis.astype(jnp.bfloat16), got_track, first_slot, first_slot + partner_give, half_slots
    )
    returned_set = partner_2(helped, "slab", swap_bit)
    own_part = grid_range(stokes_vis, tracks, 0, own_held - own_give, SLOTS)
    subgrids = own_part + lax.dynamic_update_slice_in_dim(
        jnp.zeros_like(own_part), returned_set, own_start, 1
    )
    weight_flat = pixel_weight.reshape(pixel_area)
    sub_re = (subgrids[0] * weight_flat).reshape(SLOTS, SUB, SUB)
    sub_im = (subgrids[1] * weight_flat).reshape(SLOTS, SUB, SUB)
    uv_re, uv_im = subgrid_transform(sub_re, sub_im, dft_pair)
    uv_blocks = jnp.stack([uv_re, uv_im])
    own_offsets = lax.dynamic_slice_in_dim(offsets, slab_index * SLOTS, SLOTS, 1)
    own_rows = own_offsets[0] - slab_index * rows_local
    own_cols = own_offsets[1]
    window = jnp.zeros((2, rows_local + SUB, G), jnp.float32)
    window = place_blocks(window, uv_blocks, own_rows, own_cols)
    lower_rows = passed_along(window[:, rows_local:], "slab", 1)
    slab_grid = window[:, :rows_local].at[:, :SUB].add(lower_rows)
    small_side = G // 128
    large_side = 128
    table_small = dft_table(small_side)
    table_large = dft_table(large_side)
    twiddle = twiddle_table(small_side, large_side, G)
    plane_re = slab_grid[0].reshape(rows_local, small_side, large_side)
    plane_im = slab_grid[1].reshape(rows_local, small_side, large_side)
    step_re, step_im = complex_einsum("rkc,kx->rxc", (plane_re, plane_im), table_small)
    step_re, step_im = complex_multiply((step_re, step_im), twiddle)
    step_re, step_im = complex_einsum("rxc,cb->bxr", (step_re, step_im), table_large)
    moved_block = lax.all_to_all(
        jnp.stack([step_re, step_im]), "slab", split_axis=1, concat_axis=3, tiled=True
    )
    line_re = moved_block[0].reshape(rows_local, large_side, small_side)
    line_im = moved_block[1].reshape(rows_local, large_side, small_side)
    line_re, line_im = complex_einsum("xab,ay->xby", (line_re, line_im), table_large)
    line_re, line_im = complex_multiply((line_re, line_im), twiddle)
    line_re, line_im = complex_einsum("xby,bz->xzy", (line_re, line_im), table_small)
    norm_scale = 1.0 / (SUB * SUB * math.sqrt(VIS * SLOTS * slab_count / 8.0))
    sky_re = line_re.reshape(rows_local, G) * norm_scale
    sky_im = line_im.reshape(rows_local, G) * norm_scale
    return jnp.stack([sky_re, sky_im])[:, None]


def solution(mesh):
    in_specs = (P(None, "pol", "slab", None), P(None, "slab", None), P("slab"), P(), P(), P())
    out_specs = P(None, "pol", "slab", None)
    return jax.shard_map(
        on_device, mesh=mesh, in_specs=in_specs, out_specs=out_specs, check_vma=False
    )
```

profile of v0, /device:TPU:0, one launch (start us, length us, event | category | flops | bytes accessed | tf_op | source)
XLA Modules:
  0.0 1719.4 jit_solution(8754197887101331359)
XLA Ops:
  8.9 9.3 all_gather.3
  21.9 55.4 %while.41 = (s32[]{:T(128)}, f32[2,64,1024]{2,0,1:T(2,128)S(1)}, s32[]{:T(128)}, bf16[2,64,256]{2,0,1:T(2,128)(2,1)S(1)}, f32[3,64,256]{2,1,0:T(8,128)}, /*index=5*/s32[]{:T(128)}, s32[]{:T(128)}, s32[]{:T(128)}, s32[]{}, s32[]{}) while((s32[]{:T(128)}, f32[2,64,1024]{2,0,1:T(2,128)S(1)}, s32[]{:T(128)}, ...), condition=%wide.region_5.6_spmd.clone, body=%wide.region_4.5_spmd.clone.sunk | while | flops 6330119 | bytes 2189499 | solution.py:155
  102.5 8.4 broadcast_in_dim.15
  110.8 572.1 %while.40 = (s32[]{:T(128)}, f32[2,544,4096]{2,1,0:T(8,128)}, s32[64]{0:T(128)S(1)}, s32[64]{0:T(128)S(1)}, f32[2,64,32,32]{3,2,0,1:T(8,128)S(1)}, /*index=5*/s32[]{:T(128)}, s32[]{:T(128)}, s32[]{:T(128)}, s32[]{:T(128)}) while((s32[]{:T(128)}, f32[2,544,4096]{2,1,0:T(8,128)}, s32[64]{0:T(128)S(1)}, s32[64]{0:T(128)S(1)}, ...), condition=%wide.region_9.10_spmd, body=%wide.region_8.9_spmd.sunk | while | flops 2056 | bytes 41169 | solution.py:113
  684.2 88.0 %collective-permute-start.3 = (f32[2,32,4096]{2,1,0:T(8,128)S(1)}, f32[2,32,4096]{2,1,0:T(8,128)S(1)}, u32[]{:S(2)}, u32[]{:S(2)}) collective-permute-start(f32[2,32,4096]{2,1,0:T(8,128)S(1)} %slice.121), channel_id=1, source_target_pairs={{0,1},{1,2},{2,3},{3,4},{4,5},{5,6},{6,7},{8,9},{9,10},{10,11},{11... | collective-permute-start | bytes 3145736 | tf_op jit(solution)/shard_map/ppermute | solution.py:33
  772.3 6.7 slice.119
  792.1 9.4 fusion.161
  801.5 9.6 fusion.148
  813.0 9.5 fusion.146
  822.6 19.0 %subtract_bitcast_fusion.1 = (f32[512,32,128]{2,1,0:T(8,128)}, f32[512,32,128]{2,1,0:T(8,128)}) fusion(f32[32,128]{1,0:T(8,128)S(1)} %get-tuple-element.353, f32[32,128]{1,0:T(8,128)S(1)} %get-tuple-element.354, f32[32,512,128]{2,0,1:T(8,128)} %fusion.146, f32[32,512,128]{2,0,1:T(8,128)} %fusion.161, f32[32,512,128]{2,0,1:T(8,128)} %fusion.148, ...), kind=kOutput, calls=%fused_computation.98 | convolution fusion | flops 822097920 | bytes 50364416 | tf_op jit(solution)/shard_map/rkc,kx->rxc/dot_general | solution.py:83
  841.5 23.5 %fusion.63 = f32[128,512,32]{1,0,2:T(8,128)S(1)} fusion(f32[512,32,128]{2,1,0:T(8,128)} %get-tuple-element.340), kind=kOutput, calls=%fused_computation.99 | convolution fusion | flops 3221454848 | bytes 16777216 | tf_op jit(solution)/shard_map/rxc,cb->bxr/dot_general | solution.py:86
  865.1 14.1 fusion.65
  879.1 17.2 %subtract_bitcast_fusion = f32[1,128,32,512]{3,1,2,0:T(8,128)} fusion(f32[128,512,32]{1,0,2:T(8,128)} %fusion.65, f32[512,32,128]{2,1,0:T(8,128)S(1)} %bitcast.219), kind=kOutput, calls=%fused_computation.96 | convolution fusion | flops 3223552000 | bytes 25165824 | tf_op jit(solution)/shard_map/rxc,cb->bxr/dot_general | solution.py:83
  896.4 14.2 add_bitcast_fusion
  910.6 7.3 pad_maximum_fusion
  918.0 16.6 copy.160
  934.5 416.9 %all_to_all.15 = f32[2,128,32,512]{3,2,0,1:T(8,128)S(1)} all-to-all(f32[2,128,32,512]{3,2,0,1:T(8,128)S(1)} %copy.160), channel_id=1, replica_groups=mesh['pol'=4,'slab'=8] {'slab'}, dimensions={1} | all-to-all | bytes 33554432 | tf_op jit(solution)/shard_map/all_to_all | solution.py:200
  1351.4 10.4 copy.247
  1361.9 6.9 fusion.295
  1368.8 20.9 %reshape_squeeze.15 = f32[512,128,32]{2,1,0:T(8,128)} reshape(f32[1,16,32,8,512]{4,3,2,1,0:T(8,128)} %get-tuple-element.341) | data formatting | bytes 16777216 | tf_op jit(solution)/shard_map/reshape;squeeze | solution.py:204
  1389.6 57.7 %fusion.112 = f32[512,32,128]{2,1,0:T(8,128)} fusion(f32[512,128,32]{2,1,0:T(8,128)} %reshape_squeeze.15), kind=kOutput, calls=%fused_computation.159 | convolution fusion | flops 3221454848 | bytes 16777216 | tf_op jit(solution)/shard_map/xab,ay->xby/dot_general | solution.py:86
  1447.4 58.0 %fusion.106 = f32[512,32,128]{2,1,0:T(8,128)} fusion(f32[512,128,32]{2,1,0:T(8,128)} %reshape_squeeze.15), kind=kOutput, calls=%fused_computation.151 | convolution fusion | flops 3221454848 | bytes 16777216 | tf_op jit(solution)/shard_map/xab,ay->xby/dot_general | solution.py:83
  1505.3 20.9 %reshape_squeeze.14 = f32[512,128,32]{2,1,0:T(8,128)} reshape(f32[1,16,32,8,512]{4,3,2,1,0:T(8,128)} %get-tuple-element.342) | data formatting | bytes 16777216 | tf_op jit(solution)/shard_map/reshape;squeeze | solution.py:203
  1526.2 57.7 %fusion.114 = f32[512,32,128]{2,1,0:T(8,128)} fusion(f32[512,128,32]{2,1,0:T(8,128)} %reshape_squeeze.14), kind=kOutput, calls=%fused_computation.161 | convolution fusion | flops 3221454848 | bytes 16777216 | tf_op jit(solution)/shard_map/xab,ay->xby/dot_general | solution.py:83
  1583.9 62.4 %multiply_add_fusion = (f32[512,32,128]{2,1,0:T(8,128)}, f32[512,32,128]{2,1,0:T(8,128)}) fusion(f32[32,128]{1,0:T(8,128)S(1)} %get-tuple-element.353, f32[32,128]{1,0:T(8,128)S(1)} %get-tuple-element.354, f32[512,32,128]{2,1,0:T(8,128)} %fusion.112, f32[512,32,128]{2,1,0:T(8,128)} %fusion.114, f32[512,32,128]{2,1,0:T(8,128)} %fusion.106, ...), kind=kOutput, calls=%fused_computation.93 | convolution fusion | flops 3238232064 | bytes 50364416 | tf_op jit(solution)/shard_map/xab,ay->xby/dot_general | solution.py:86
  1646.3 10.9 fusion.143
  1657.3 9.6 fusion.159
  1666.8 11.4 multiply_bitcast_fusion.1
  1678.2 10.4 multiply_bitcast_fusion
  1688.7 9.4 mul.577
  1698.1 9.4 mul.574
  1707.5 11.8 maximum_bitcast_fusion.2
  (402 shorter events, 443.1 us)
Async XLA Ops:
  0.0 77.3 %copy-start = (s32[2,512]{1,0:T(2,128)S(1)}, s32[2,512]{1,0:T(2,128)}, u32[]{:S(2)}) copy-start(s32[2,512]{1,0:T(2,128)} %param.19) | copy-start | bytes 12292
  4.8 73.8 %collective-permute-start.1 = (f32[3,32,256]{2,1,0:T(8,128)S(1)}, f32[3,32,256]{2,1,0:T(8,128)S(1)}, u32[]{:S(2)}, u32[]{:S(2)}) collective-permute-start(f32[3,32,256]{2,1,0:T(8,128)S(1)} %constant_dynamic-slice_fusion.4), channel_id=1, source_target_pairs={{0,4},{1,5},{2,6},{3,7},{4,0},{5,1},{6,2},{7,3},{8,12},{9,13},{10,... | collective-permute-start | bytes 294920 | tf_op jit(solution)/shard_map/ppermute | solution.py:27
  21.2 57.3 %collective-permute-start = (bf16[2,32,256]{2,1,0:T(8,128)(2,1)S(1)}, bf16[2,32,256]{2,1,0:T(8,128)(2,1)S(1)}, u32[]{:S(2)}, u32[]{:S(2)}) collective-permute-start(bf16[2,32,256]{2,1,0:T(8,128)(2,1)S(1)} %dynamic-slice_convert_fusion), channel_id=1, source_target_pairs={{0,4},{1,5},{2,6},{3,7},{4,0},{5,1},{6,2},{7,3},{8,12},{9,13},{10,... | collective-permute-start | bytes 98312 | tf_op jit(solution)/shard_map/ppermute | solution.py:27
  78.9 14.3 copy-start.5
  78.9 7.3 collective-permute-start.2
  684.2 94.7 %collective-permute-start.3 = (f32[2,32,4096]{2,1,0:T(8,128)S(1)}, f32[2,32,4096]{2,1,0:T(8,128)S(1)}, u32[]{:S(2)}, u32[]{:S(2)}) collective-permute-start(f32[2,32,4096]{2,1,0:T(8,128)S(1)} %slice.121), channel_id=1, source_target_pairs={{0,1},{1,2},{2,3},{3,4},{4,5},{5,6},{6,7},{8,9},{9,10},{10,11},{11... | collective-permute-start | bytes 3145736 | tf_op jit(solution)/shard_map/ppermute | solution.py:33
  792.1 19.1 %slice-start.4 = ((s8[8388608]{0:T(1024)(128)(4,1)}), s8[4194304]{0:T(1024)(128)(4,1)S(1)}, s32[]{:S(2)}) async-start(s8[8388608]{0:T(1024)(128)(4,1)} %bitcast.226), calls=%async_computation.5 | async-start | bytes 8388608
  801.5 9.7 slice-start.5
  813.0 9.5 copy-start.3
  841.5 23.5 %copy-start.4 = (f32[512,32,128]{2,1,0:T(8,128)S(1)}, f32[512,32,128]{2,1,0:T(8,128)}, u32[]{:S(2)}) copy-start(f32[512,32,128]{2,1,0:T(8,128)} %get-tuple-element.340) | copy-start | bytes 25165828
  841.5 37.6 %slice-start.2 = ((s8[8388608]{0:T(1024)(128)(4,1)}), s8[4194304]{0:T(1024)(128)(4,1)S(1)}, s32[]{:S(2)}) async-start(s8[8388608]{0:T(1024)(128)(4,1)} %bitcast.218), calls=%async_computation.3 | async-start | bytes 8388608
  865.0 14.1 slice-start.3
  1646.3 10.9 copy-start.2
  1646.3 20.5 %slice-start = ((s8[8388608]{0:T(1024)(128)(4,1)}), s8[4194304]{0:T(1024)(128)(4,1)S(1)}, s32[]{:S(2)}) async-start(s8[8388608]{0:T(1024)(128)(4,1)} %bitcast.216), calls=%async_computation.1 | async-start | bytes 8388608
  1657.2 9.6 slice-start.1
  1707.5 11.8 copy-start.1
where the time goes:
time: 1750 us; the launch traced here: 1720 us
  blocking collectives  426 us (24%)
  local copies, waits for them, and re-layouts  409 us (23%)
  matrix products  406 us (23%)
  loops' own time  235 us (13%)
  other arithmetic  139 us (8%)
  starting transfers between devices  93.4 us (5%)
    all_to_all x1, blocking collectives, on_device(): lax.all_to_all(jnp.stack([step_re, step_im]), 'slab', split_axis=1, conca...  417 us
    another operation x1, loops' own time, place_blocks(): return lax.fori_loop(0, block_count, add_one, window)  234 us
    dynamic_update_slice x64, local copies, waits for them, and re-layouts, add_one(): return lax.dynamic_update_slice(current_window, current + block, corner)  196 us
    dot_general x6, matrix products, complex_einsum(): jnp.einsum(pattern, left_re, right_re, precision=highest)  105 us
    dot_general x6, matrix products, complex_einsum(): jnp.einsum(pattern, left_im, right_re, precision=highest)  103 us
    dot_general x6, matrix products, complex_einsum(): jnp.einsum(pattern, left_re, right_im, precision=highest)  98.9 us
    dot_general x6, matrix products, complex_einsum(): jnp.einsum(pattern, left_im, right_im, precision=highest)  94.9 us
    ppermute x1, starting transfers between devices, passed_along(): return lax.ppermute(value, axis, pairs)  88 us
  transfers between devices with their start and end apart: 4, of which 1 were waited for; matrix products, arithmetic and copies ran while one was open for 4% of the time, Pallas kernels for 0%

commit v1 on v0

--- a/solution.py
+++ b/solution.py
@@ -21,6 +21,29 @@
     [[0.0, 0.0, 0.0, 0.0], [0.0, 0.0, 0.0, 0.0], [0.0, 0.0, 0.0, 0.0], [0.0, -0.5, 0.5, 0.0]],
     np.float32,
 )
+
+
+def cut_along(x, dim, count):
+    shape = x.shape
+    pieces = x.reshape(*shape[:dim], count, shape[dim] // count, *shape[dim + 1 :])
+    return jnp.moveaxis(pieces, dim, 0)
+
+
+def laid_out(pieces, dim):
+    shape = list(pieces.shape[1:])
+    shape[dim] *= pieces.shape[0]
+    return jnp.moveaxis(pieces, 0, dim).reshape(shape)
+
+
+def swapped_with_each(array, axis, split_dim, concat_dim):
+    size, index = (lax.axis_size(axis), lax.axis_index(axis))
+    blocks = cut_along(array, split_dim, size)
+    finished = [blocks[index]]
+    for step in range(1, size):
+        sent = blocks[index ^ step]
+        finished.append(lax.ppermute(sent, axis, [(i, i ^ step) for i in range(size)]))
+    blocks = jnp.stack(finished)[index ^ jnp.arange(size)]
+    return laid_out(blocks, concat_dim)
 
 
 def partner_2(value, axis, distance):
@@ -197,9 +220,7 @@
     step_re, step_im = complex_einsum("rkc,kx->rxc", (plane_re, plane_im), table_small)
     step_re, step_im = complex_multiply((step_re, step_im), twiddle)
     step_re, step_im = complex_einsum("rxc,cb->bxr", (step_re, step_im), table_large)
-    moved_block = lax.all_to_all(
-        jnp.stack([step_re, step_im]), "slab", split_axis=1, concat_axis=3, tiled=True
-    )
+    moved_block = swapped_with_each(jnp.stack([step_re, step_im]), "slab", 1, 3)
     line_re = moved_block[0].reshape(rows_local, large_side, small_side)
     line_im = moved_block[1].reshape(rows_local, large_side, small_side)
     line_re, line_im = complex_einsum("xab,ay->xby", (line_re, line_im), table_large)

time: 1750 us -> 1810 us (1.034)
  the two profiles are of different devices: /device:TPU:0 before, /device:TPU:17 now
where the time goes in v1:
time: 1810 us; the launch traced here: 1780 us
  local copies, waits for them, and re-layouts  460 us (25%)
  matrix products  427 us (24%)
  waiting for transfers between devices  341 us (19%)
  loops' own time  264 us (15%)
  other arithmetic  204 us (11%)
  starting transfers between devices  75.2 us (4%)
    ppermute x7, waiting for transfers between devices, swapped_with_each(): lax.ppermute(sent, axis, [(i, i ^ step) for i in range(size)])  333 us
    another operation x1, loops' own time, place_blocks(): return lax.fori_loop(0, block_count, add_one, window)  261 us
    dynamic_update_slice x64, local copies, waits for them, and re-layouts, add_one(): return lax.dynamic_update_slice(current_window, current + block, corner)  195 us
    another operation x26, other arithmetic  116 us
    dot_general x6, matrix products, complex_einsum(): jnp.einsum(pattern, left_re, right_re, precision=highest)  114 us
    dot_general x6, matrix products, complex_einsum(): jnp.einsum(pattern, left_re, right_im, precision=highest)  107 us
    dot_general x6, matrix products, complex_einsum(): jnp.einsum(pattern, left_im, right_re, precision=highest)  105 us
    dot_general x6, matrix products, complex_einsum(): jnp.einsum(pattern, left_im, right_im, precision=highest)  93.2 us
  transfers between devices with their start and end apart: 11, of which 7 were waited for; matrix products, arithmetic and copies ran while one was open for 3% of the time, Pallas kernels for 0%

profile of v1, /device:TPU:17, one launch (start us, length us, event | category | flops | bytes accessed | tf_op | source)
XLA Modules:
  0.0 1782.1 jit_solution(9937940997302744913)
XLA Ops:
  25.2 124.7 %while.42 = (s32[]{:T(128)}, f32[2,32,1024]{2,1,0:T(8,128)S(1)}, s32[]{:T(128)}, bf16[2,32,256]{2,0,1:T(2,128)(2,1)S(1)}, f32[3,32,256]{2,1,0:T(8,128)S(1)}, /*index=5*/s32[]{:T(128)}, s32[]{:T(128)}, s32[]{:T(128)}, s32[]{}, s32[]{}) while((s32[]{:T(128)}, f32[2,32,1024]{2,1,0:T(8,128)S(1)}, s32[]{:T(128)}, ...), condition=%wide.region_7.8_spmd.clone, body=%wide.region_6.7_spmd.clone.sunk | while | flops 6330119 | bytes 2222259 | solution.py:178
  149.9 14.6 collective-permute-start.2
  192.9 602.2 %while.40 = (s32[]{:T(128)}, f32[2,544,4096]{2,1,0:T(8,128)}, s32[64]{0:T(128)S(1)}, s32[64]{0:T(128)S(1)}, f32[2,64,32,32]{3,2,0,1:T(8,128)S(1)}, /*index=5*/s32[]{:T(128)}, s32[]{:T(128)}, s32[]{:T(128)}, s32[]{:T(128)}) while((s32[]{:T(128)}, f32[2,544,4096]{2,1,0:T(8,128)}, s32[64]{0:T(128)S(1)}, s32[64]{0:T(128)S(1)}, ...), condition=%wide.region_9.10_spmd, body=%wide.region_8.9_spmd.sunk | while | flops 2056 | bytes 41161 | solution.py:136
  796.4 50.1 %collective-permute-start.3 = (f32[2,32,4096]{2,1,0:T(8,128)S(1)}, f32[2,32,4096]{2,1,0:T(8,128)S(1)}, u32[]{:S(2)}, u32[]{:S(2)}) collective-permute-start(f32[2,32,4096]{2,1,0:T(8,128)S(1)} %slice.121), channel_id=1, source_target_pairs={{0,1},{1,2},{2,3},{3,4},{4,5},{5,6},{6,7},{8,9},{9,10},{10,11},{11... | collective-permute-start | bytes 3145736 | tf_op jit(solution)/shard_map/ppermute | solution.py:56
  870.7 9.5 fusion.158
  880.3 9.6 fusion.171
  891.8 9.5 fusion.156
  901.3 19.3 %subtract_bitcast_fusion = (f32[512,32,128]{2,1,0:T(8,128)}, f32[512,32,128]{2,1,0:T(8,128)}) fusion(f32[32,128]{1,0:T(8,128)S(1)} %get-tuple-element.361, f32[32,128]{1,0:T(8,128)S(1)} %get-tuple-element.362, f32[32,512,128]{2,0,1:T(8,128)} %fusion.156, f32[32,512,128]{2,0,1:T(8,128)} %fusion.171, f32[32,512,128]{2,0,1:T(8,128)} %fusion.158, ...), kind=kOutput, calls=%fused_computation.111 | convolution fusion | flops 822097920 | bytes 50364416 | tf_op jit(solution)/shard_map/rkc,kx->rxc/dot_general | solution.py:106
  920.6 22.3 %fusion.63 = f32[128,512,32]{1,0,2:T(8,128)} fusion(f32[512,32,128]{2,1,0:T(8,128)} %get-tuple-element.340), kind=kOutput, calls=%fused_computation.112 | convolution fusion | flops 3221454848 | bytes 16777216 | tf_op jit(solution)/shard_map/rxc,cb->bxr/dot_general | solution.py:109
  942.9 13.7 fusion.65
  956.6 23.5 %fusion.74 = f32[128,512,32]{1,0,2:T(8,128)S(1)} fusion(f32[128,512,32]{1,0,2:T(8,128)} %fusion.63, f32[512,32,128]{2,1,0:T(8,128)S(1)} %bitcast.257), kind=kOutput, calls=%fused_computation.121 | convolution fusion | flops 3223552000 | bytes 25165824 | tf_op jit(solution)/shard_map/rxc,cb->bxr/dot_general | solution.py:109
  980.1 24.2 %fusion.71 = f32[128,512,32]{1,0,2:T(8,128)S(1)} fusion(f32[128,512,32]{1,0,2:T(8,128)} %fusion.65, f32[512,32,128]{2,1,0:T(8,128)} %get-tuple-element.339), kind=kOutput, calls=%fused_computation.120 | convolution fusion | flops 3223552000 | bytes 25165824 | tf_op jit(solution)/shard_map/rxc,cb->bxr/dot_general | solution.py:106
  1030.7 112.6 %collective-permute-done.5 = f32[2,16,32,512]{3,2,1,0:T(8,128)} collective-permute-done((f32[2,16,32,512]{3,2,1,0:T(8,128)}, f32[2,16,32,512]{3,2,1,0:T(8,128)}, u32[]{:S(2)}, u32[]{:S(2)}) %collective-permute-start.5) | collective-permute-done | bytes 2097184 | tf_op jit(solution)/shard_map/ppermute | solution.py:44
  1154.5 33.8 %collective-permute-done.6 = f32[2,16,32,512]{3,2,1,0:T(8,128)} collective-permute-done((f32[2,16,32,512]{3,2,1,0:T(8,128)}, f32[2,16,32,512]{3,2,1,0:T(8,128)}, u32[]{:S(2)}, u32[]{:S(2)}) %collective-permute-start.6) | collective-permute-done | bytes 2097184 | tf_op jit(solution)/shard_map/ppermute | solution.py:44
  1195.0 95.9 %collective-permute-done.8 = f32[2,16,32,512]{3,2,1,0:T(8,128)S(1)} collective-permute-done((f32[2,16,32,512]{3,2,1,0:T(8,128)S(1)}, f32[2,16,32,512]{3,2,1,0:T(8,128)S(1)}, u32[]{:S(2)}, u32[]{:S(2)}) %collective-permute-start.8) | collective-permute-done | bytes 2097184 | tf_op jit(solution)/shard_map/ppermute | solution.py:44
  1292.4 47.0 %collective-permute-done.9 = f32[2,16,32,512]{3,2,1,0:T(8,128)S(1)} collective-permute-done((f32[2,16,32,512]{3,2,1,0:T(8,128)S(1)}, f32[2,16,32,512]{3,2,1,0:T(8,128)S(1)}, u32[]{:S(2)}, u32[]{:S(2)}) %collective-permute-start.9) | collective-permute-done | bytes 2097184 | tf_op jit(solution)/shard_map/ppermute | solution.py:44
  1340.9 43.8 %collective-permute-done.10 = f32[2,16,32,512]{3,2,1,0:T(8,128)S(1)} collective-permute-done((f32[2,16,32,512]{3,2,1,0:T(8,128)S(1)}, f32[2,16,32,512]{3,2,1,0:T(8,128)S(1)}, u32[]{:S(2)}, u32[]{:S(2)}) %collective-permute-start.10) | collective-permute-done | bytes 2097184 | tf_op jit(solution)/shard_map/ppermute | solution.py:44
  1386.3 13.8 gather_fusion
  1409.4 9.7 copy.186
  1419.1 20.8 %reshape_squeeze.15 = f32[512,128,32]{2,1,0:T(8,128)} reshape(f32[1,16,32,8,512]{4,3,2,1,0:T(8,128)} %copy.186) | data formatting | bytes 16777216 | tf_op jit(solution)/shard_map/reshape;squeeze | solution.py:225
  1440.0 57.9 %fusion.116 = f32[512,32,128]{2,1,0:T(8,128)} fusion(f32[512,128,32]{2,1,0:T(8,128)} %reshape_squeeze.15), kind=kOutput, calls=%fused_computation.189 | convolution fusion | flops 3221454848 | bytes 16777216 | tf_op jit(solution)/shard_map/xab,ay->xby/dot_general | solution.py:106
  1497.9 58.3 %fusion.122 = f32[512,32,128]{2,1,0:T(8,128)} fusion(f32[512,128,32]{2,1,0:T(8,128)} %reshape_squeeze.15), kind=kOutput, calls=%fused_computation.197 | convolution fusion | flops 3221454848 | bytes 16777216 | tf_op jit(solution)/shard_map/xab,ay->xby/dot_general | solution.py:109
  1556.2 9.9 copy.184
  1566.1 20.8 %reshape_squeeze.14 = f32[512,128,32]{2,1,0:T(8,128)} reshape(f32[1,16,32,8,512]{4,3,2,1,0:T(8,128)} %copy.184) | data formatting | bytes 16777216 | tf_op jit(solution)/shard_map/reshape;squeeze | solution.py:224
  1586.9 57.7 %fusion.124 = f32[512,32,128]{2,1,0:T(8,128)} fusion(f32[512,128,32]{2,1,0:T(8,128)} %reshape_squeeze.14), kind=kOutput, calls=%fused_computation.199 | convolution fusion | flops 3221454848 | bytes 16777216 | tf_op jit(solution)/shard_map/xab,ay->xby/dot_general | solution.py:106
  1644.6 62.4 %multiply_add_fusion = (f32[512,32,128]{2,1,0:T(8,128)}, f32[512,32,128]{2,1,0:T(8,128)}) fusion(f32[32,128]{1,0:T(8,128)S(1)} %copy-done.10, f32[32,128]{1,0:T(8,128)S(1)} %copy-done.12, f32[512,32,128]{2,1,0:T(8,128)} %fusion.122, f32[512,32,128]{2,1,0:T(8,128)} %fusion.124, f32[512,32,128]{2,1,0:T(8,128)} %fusion.116, f32[512,128,32]{2,1,0:T(8,128)} %reshape_squeeze.14), kind=kOutput, calls=%fused_computation.108 | convolution fusion | flops 3238232064 | bytes 50364416 | tf_op jit(solution)/shard_map/xab,ay->xby/dot_general | solution.py:109
  1707.0 11.0 fusion.169
  1718.1 9.5 fusion.153
  1727.6 10.3 multiply_bitcast_fusion.1
  1737.8 9.6 mul.574
  1747.4 13.3 multiply_bitcast_fusion
  1770.1 11.8 maximum_bitcast_fusion.2
  (615 shorter events, 613.3 us)
Async XLA Ops:
  0.0 23.8 %copy-start = (s32[2,512]{1,0:T(2,128)S(1)}, s32[2,512]{1,0:T(2,128)}, u32[]{:S(2)}) copy-start(s32[2,512]{1,0:T(2,128)} %param.19) | copy-start | bytes 12292
  14.6 10.5 collective-permute-start
  15.6 9.6 collective-permute-start.1
  149.9 25.3 %copy-start.8 = (f32[32,32]{1,0:T(8,128)S(1)}, f32[32,32]{1,0:T(8,128)}, u32[]{:S(2)}) copy-start(f32[32,32]{1,0:T(8,128)} %param.21) | copy-start | bytes 12292
  149.9 18.4 %collective-permute-start.2 = (f32[2,32,1024]{2,1,0:T(8,128)S(1)}, f32[2,32,1024]{2,1,0:T(8,128)S(1)}, u32[]{:S(2)}, u32[]{:S(2)}) collective-permute-start(f32[2,32,1024]{2,1,0:T(8,128)S(1)} %get-tuple-element.198), channel_id=1, source_target_pairs={{0,4},{1,5},{2,6},{3,7},{4,0},{5,1},{6,2},{7,3},{8,12},{9,13},{10,... | collective-permute-start | bytes 786440 | tf_op jit(solution)/shard_map/ppermute | solution.py:50
  796.4 61.3 %collective-permute-start.3 = (f32[2,32,4096]{2,1,0:T(8,128)S(1)}, f32[2,32,4096]{2,1,0:T(8,128)S(1)}, u32[]{:S(2)}, u32[]{:S(2)}) collective-permute-start(f32[2,32,4096]{2,1,0:T(8,128)S(1)} %slice.121), channel_id=1, source_target_pairs={{0,1},{1,2},{2,3},{3,4},{4,5},{5,6},{6,7},{8,9},{9,10},{10,11},{11... | collective-permute-start | bytes 3145736 | tf_op jit(solution)/shard_map/ppermute | solution.py:56
  846.6 54.7 %copy-start.9 = (f32[32,128]{1,0:T(8,128)}, f32[32,128]{1,0:T(8,128)S(1)}, u32[]{:S(2)}) copy-start(f32[32,128]{1,0:T(8,128)S(1)} %get-tuple-element.361) | copy-start | bytes 49156
  846.6 54.7 %copy-start.11 = (f32[32,128]{1,0:T(8,128)}, f32[32,128]{1,0:T(8,128)S(1)}, u32[]{:S(2)}) copy-start(f32[32,128]{1,0:T(8,128)S(1)} %get-tuple-element.362) | copy-start | bytes 49156
  870.7 19.2 %slice-start.6 = ((s8[8388608]{0:T(1024)(128)(4,1)}), s8[4194304]{0:T(1024)(128)(4,1)S(1)}, s32[]{:S(2)}) async-start(s8[8388608]{0:T(1024)(128)(4,1)} %bitcast.265), calls=%async_computation.6 | async-start | bytes 8388608
  880.3 9.7 slice-start.7
  891.8 9.5 copy-start.5
  920.6 22.4 %copy-start.6 = (f32[512,32,128]{2,1,0:T(8,128)S(1)}, f32[512,32,128]{2,1,0:T(8,128)}, u32[]{:S(2)}) copy-start(f32[512,32,128]{2,1,0:T(8,128)} %get-tuple-element.340) | copy-start | bytes 25165828
  920.6 36.0 %slice-start.2 = ((s8[8388608]{0:T(1024)(128)(4,1)}), s8[4194304]{0:T(1024)(128)(4,1)S(1)}, s32[]{:S(2)}) async-start(s8[8388608]{0:T(1024)(128)(4,1)} %bitcast.256), calls=%async_computation.2 | async-start | bytes 8388608
  942.9 13.7 slice-start.3
  980.1 24.3 %copy-start.2 = (f32[128,512,32]{1,0,2:T(8,128)}, f32[128,512,32]{1,0,2:T(8,128)S(1)}, u32[]{:S(2)}) copy-start(f32[128,512,32]{1,0,2:T(8,128)S(1)} %fusion.74) | copy-start | bytes 25165828
  1004.3 4.0 copy-start.3
  1011.0 18.3 %collective-permute-start.4 = (f32[2,16,32,512]{3,2,1,0:T(8,128)}, f32[2,16,32,512]{3,2,1,0:T(8,128)}, u32[]{:S(2)}, u32[]{:S(2)}) collective-permute-start(f32[2,16,32,512]{3,2,1,0:T(8,128)} %bitcast.223), channel_id=1, source_target_pairs={{0,1},{1,0},{2,3},{3,2},{4,5},{5,4},{6,7},{7,6},{8,9},{9,8},{10,11... | collective-permute-start | bytes 6291464 | tf_op jit(solution)/shard_map/ppermute | solution.py:44
  1013.5 129.8 %collective-permute-start.5 = (f32[2,16,32,512]{3,2,1,0:T(8,128)}, f32[2,16,32,512]{3,2,1,0:T(8,128)}, u32[]{:S(2)}, u32[]{:S(2)}) collective-permute-start(f32[2,16,32,512]{3,2,1,0:T(8,128)} %bitcast.222), channel_id=1, source_target_pairs={{0,2},{1,3},{2,0},{3,1},{4,6},{5,7},{6,4},{7,5},{8,10},{9,11},{10,... | collective-permute-start | bytes 6291464 | tf_op jit(solution)/shard_map/ppermute | solution.py:44
  1018.6 169.6 %collective-permute-start.6 = (f32[2,16,32,512]{3,2,1,0:T(8,128)}, f32[2,16,32,512]{3,2,1,0:T(8,128)}, u32[]{:S(2)}, u32[]{:S(2)}) collective-permute-start(f32[2,16,32,512]{3,2,1,0:T(8,128)} %bitcast.221), channel_id=1, source_target_pairs={{0,3},{1,2},{2,1},{3,0},{4,7},{5,6},{6,5},{7,4},{8,11},{9,10},{10,... | collective-permute-start | bytes 6291464 | tf_op jit(solution)/shard_map/ppermute | solution.py:44
  1021.2 170.2 %collective-permute-start.7 = (f32[2,16,32,512]{3,2,1,0:T(8,128)}, f32[2,16,32,512]{3,2,1,0:T(8,128)}, u32[]{:S(2)}, u32[]{:S(2)}) collective-permute-start(f32[2,16,32,512]{3,2,1,0:T(8,128)} %bitcast.220), channel_id=1, source_target_pairs={{0,4},{1,5},{2,6},{3,7},{4,0},{5,1},{6,2},{7,3},{8,12},{9,13},{10,... | collective-permute-start | bytes 6291464 | tf_op jit(solution)/shard_map/ppermute | solution.py:44
  1023.8 5.6 copy-start.7
  1025.1 265.8 %collective-permute-start.8 = (f32[2,16,32,512]{3,2,1,0:T(8,128)S(1)}, f32[2,16,32,512]{3,2,1,0:T(8,128)S(1)}, u32[]{:S(2)}, u32[]{:S(2)}) collective-permute-start(f32[2,16,32,512]{3,2,1,0:T(8,128)S(1)} %bitcast.271), channel_id=1, source_target_pairs={{0,5},{1,4},{2,7},{3,6},{4,1},{5,0},{6,3},{7,2},{8,13},{9,12},{10,... | collective-permute-start | bytes 6291464 | tf_op jit(solution)/shard_map/ppermute | solution.py:44
  1029.3 310.1 %collective-permute-start.9 = (f32[2,16,32,512]{3,2,1,0:T(8,128)S(1)}, f32[2,16,32,512]{3,2,1,0:T(8,128)S(1)}, u32[]{:S(2)}, u32[]{:S(2)}) collective-permute-start(f32[2,16,32,512]{3,2,1,0:T(8,128)S(1)} %bitcast.272), channel_id=1, source_target_pairs={{0,6},{1,7},{2,4},{3,5},{4,2},{5,3},{6,0},{7,1},{8,14},{9,15},{10,... | collective-permute-start | bytes 6291464 | tf_op jit(solution)/shard_map/ppermute | solution.py:44
  1143.3 241.5 %collective-permute-start.10 = (f32[2,16,32,512]{3,2,1,0:T(8,128)S(1)}, f32[2,16,32,512]{3,2,1,0:T(8,128)S(1)}, u32[]{:S(2)}, u32[]{:S(2)}) collective-permute-start(f32[2,16,32,512]{3,2,1,0:T(8,128)S(1)} %bitcast.273), channel_id=1, source_target_pairs={{0,7},{1,6},{2,5},{3,4},{4,3},{5,2},{6,1},{7,0},{8,15},{9,14},{10,... | collective-permute-start | bytes 6291464 | tf_op jit(solution)/shard_map/ppermute | solution.py:44
  1440.0 116.2 %slice-start.4 = ((s8[8388608]{0:T(1024)(128)(4,1)}), s8[4194304]{0:T(1024)(128)(4,1)S(1)}, s32[]{:S(2)}) async-start(s8[8388608]{0:T(1024)(128)(4,1)} %bitcast.263), calls=%async_computation.4 | async-start | bytes 8388608
  1497.9 58.3 %slice-start.5 = ((s8[8388608]{0:T(1024)(128)(4,1)}), s8[4194304]{0:T(1024)(128)(4,1)S(1)}, s32[]{:S(2)}) async-start(s8[8388608]{0:T(1024)(128)(4,1)} %bitcast.263), calls=%async_computation.5 | async-start | bytes 8388608
  1586.9 57.7 %copy-start.10 = (f32[32,128]{1,0:T(8,128)S(1)}, f32[32,128]{1,0:T(8,128)}, u32[]{:S(2)}) copy-start(f32[32,128]{1,0:T(8,128)} %copy-done.9) | copy-start | bytes 49156
  1586.9 57.7 %copy-start.12 = (f32[32,128]{1,0:T(8,128)S(1)}, f32[32,128]{1,0:T(8,128)}, u32[]{:S(2)}) copy-start(f32[32,128]{1,0:T(8,128)} %copy-done.11) | copy-start | bytes 49156
  1707.0 11.0 copy-start.4
  1707.0 20.5 %slice-start = ((s8[8388608]{0:T(1024)(128)(4,1)}), s8[4194304]{0:T(1024)(128)(4,1)S(1)}, s32[]{:S(2)}) async-start(s8[8388608]{0:T(1024)(128)(4,1)} %bitcast.250), calls=%async_computation | async-start | bytes 8388608
  1718.1 9.5 slice-start.1
  1770.1 11.8 copy-start.1
